TPU v7x, 256 devices: a whole 4x4x8 slice. The times are simulated.
256 devices in a mesh: frame: 16 (over x_hi, z), head: 8 (over y, core), dp: 2 (over x_lo).
Axes of the slice: x: 4 (x_hi: 2, x_lo: 2; x = x_hi * 2 + x_lo), y: 4, z: 8, core: 2. Of those that a mesh axis runs over, the one named last changes fastest.
Arguments:
- clip: bfloat16 [2, 4096, 256], P('dp', 'frame'), may hold values from -40 to 40
- block_ids: int32 [2, 4096], P('dp'), may hold values from 0 to 63, never falling along the last dimension, each value on 1 to 128 neighbouring positions
- w_spatial: bfloat16 [9, 256, 256], replicated, may hold values from -0.125 to 0.125
- w_temporal: bfloat16 [3, 256, 256], replicated, may hold values from -0.21875 to 0.21875
- w_query: bfloat16 [256, 2048], P(None, 'head'), may hold values from -0.375 to 0.375
- w_key: bfloat16 [256, 2048], P(None, 'head'), may hold values from -0.375 to 0.375
- w_value: bfloat16 [256, 2048], P(None, 'head'), may hold values from -0.375 to 0.375
- w_out: bfloat16 [2048, 256], P('head'), may hold values from -0.125 to 0.125
- cotangent: bfloat16 [2, 4096, 256], P('dp', 'frame'), may hold values from -6 to 6
Outputs:
- grad_spatial: float32 [9, 256, 256], replicated
- grad_temporal: float32 [3, 256, 256], replicated
- grad_query: float32 [256, 2048], P(None, 'head')
- grad_key: float32 [256, 2048], P(None, 'head')
- grad_value: float32 [256, 2048], P(None, 'head')
- grad_out: float32 [2048, 256], P('head')
Inputs may be any that keep to these rules, and one draw needn't show every extreme that they name: `block_ids`: block numbers never fall along a clip's tokens; every block has 1 to (128) tokens.
All inputs are finite; a program needn't handle non-finite values.
Results may differ from a plain program's by a relative error of at most 0.04.
Values may be sent and summed in bfloat16 or wider, within the bound.
No kernel may reach another device: no remote copies, remote signals or barrier semaphores. Data moves between devices by JAX's collectives and lax.ppermute only.
A program may use at most 128 MiB of HBM per device.

v0:
```python
import jax
import jax.numpy as jnp
from jax import lax
from jax.sharding import PartitionSpec as P

HD = 128
SIDE = 8
NEG_FILL = -1e30


def with_halo(cells, sides, width):
    for axis, dim in sides:
        count = lax.axis_size(axis)
        ends = count - 1
        head = lax.slice_in_dim(cells, 0, width, axis=dim)
        tail = lax.slice_in_dim(cells, cells.shape[dim] - width, cells.shape[dim], axis=dim)
        cells = jnp.concatenate(
            [
                lax.ppermute(tail, axis, [(i, (i + 1) % count) for i in range(ends)]),
                cells,
                lax.ppermute(head, axis, [((i + 1) % count, i) for i in range(ends)]),
            ],
            axis=dim,
        )
    return cells


def spatial_taps(frame_grid, side):
    padded = jnp.pad(frame_grid, ((0, 0), (1, 1), (1, 1), (0, 0)))
    count = frame_grid.shape[0] * side * side
    width = frame_grid.shape[3]
    return [
        padded[:, row_off : row_off + side, col_off : col_off + side, :].reshape(count, width)
        for row_off in range(3)
        for col_off in range(3)
    ]


def silu_slope(pre_act):
    sigma = jax.nn.sigmoid(pre_act)
    return sigma * (1.0 + pre_act * (1.0 - sigma))


def frame_rims(field):
    return with_halo(field, (("frame", 0),), SIDE * SIDE)


def take_head(matrix, which_head):
    return matrix[:, which_head * HD : (which_head + 1) * HD]


def contract_rows(left, right):
    return lax.dot_general(
        left, right, (((0,), (0,)), ((), ())), preferred_element_type=jnp.float32
    )


def on_device(clip, block_ids, w_spatial, w_temporal, w_query, w_key, w_value, w_out, cotangent):
    frames_in = clip[0]
    upstream = cotangent[0]
    clip_blocks = block_ids[0]
    tok_local, channels = frames_in.shape
    frame_len = SIDE * SIDE
    scale = HD ** (-0.5)
    grid = frames_in.reshape(tok_local // frame_len, SIDE, SIDE, channels)
    taps = spatial_taps(grid, SIDE)
    pre_act = jnp.zeros((tok_local, channels), jnp.float32)
    for offset in range(9):
        pre_act = pre_act + jnp.dot(
            taps[offset], w_spatial[offset], preferred_element_type=jnp.float32
        )
    hidden = jax.nn.silu(pre_act).astype(jnp.bfloat16)
    hidden_rim = frame_rims(hidden)
    temporal = jnp.zeros((tok_local, channels), jnp.float32)
    for offset in range(3):
        temporal = temporal + jnp.dot(
            hidden_rim[offset * frame_len : offset * frame_len + tok_local],
            w_temporal[offset],
            preferred_element_type=jnp.float32,
        )
    features = temporal.astype(jnp.bfloat16)
    queries_local = jnp.dot(features, w_query, preferred_element_type=jnp.float32).astype(
        jnp.bfloat16
    )
    keys_local = jnp.dot(features, w_key, preferred_element_type=jnp.float32).astype(jnp.bfloat16)
    values_local = jnp.dot(features, w_value, preferred_element_type=jnp.float32).astype(
        jnp.bfloat16
    )
    keys_every, values_every = (
        lax.all_gather(keys_local, "frame", axis=0, tiled=True),
        lax.all_gather(values_local, "frame", axis=0, tiled=True),
    )
    first_row = lax.axis_index("frame") * tok_local
    grad_attended = jnp.dot(upstream, w_out.T, preferred_element_type=jnp.float32).astype(
        jnp.bfloat16
    )
    queries_held, grad_held = (queries_local, grad_attended)
    held_blocks = lax.dynamic_slice_in_dim(clip_blocks, first_row, tok_local)
    visible = clip_blocks[None, :] <= held_blocks[:, None]
    heads_here = queries_local.shape[1] // HD
    width_here = queries_local.shape[1]
    attended_parts, grad_query_parts, prob_list, score_grads, norm_list, delta_list = (
        [],
        [],
        [],
        [],
        [],
        [],
    )
    for which_head in range(heads_here):
        query_head = take_head(queries_held, which_head)
        key_head = take_head(keys_every, which_head)
        value_head = take_head(values_every, which_head)
        grad_head = take_head(grad_held, which_head)
        scores = jnp.dot(query_head, key_head.T, preferred_element_type=jnp.float32) * scale
        masked = jnp.where(visible, scores, NEG_FILL)
        top = jnp.max(masked, axis=1, keepdims=True)
        total = jnp.sum(jnp.where(visible, jnp.exp(masked - top), 0.0), axis=1, keepdims=True)
        log_norm = top + jnp.log(total)
        probs = jnp.where(visible, jnp.exp(masked - log_norm), 0.0)
        probs_low = probs.astype(jnp.bfloat16)
        attended = jnp.dot(probs_low, value_head, preferred_element_type=jnp.float32).astype(
            jnp.bfloat16
        )
        delta = jnp.sum(
            grad_head.astype(jnp.float32) * attended.astype(jnp.float32), axis=1, keepdims=True
        )
        grad_probs = jnp.dot(grad_head, value_head.T, preferred_element_type=jnp.float32)
        grad_scores = (probs * (grad_probs - delta) * scale).astype(jnp.bfloat16)
        grad_query_parts.append(
            jnp.dot(grad_scores, key_head, preferred_element_type=jnp.float32).astype(jnp.bfloat16)
        )
        attended_parts.append(attended)
        prob_list.append(probs_low)
        score_grads.append(grad_scores)
        norm_list.append(log_norm)
        delta_list.append(delta)
    attended_all = jnp.concatenate(attended_parts, axis=1)
    grad_queries = jnp.concatenate(grad_query_parts, axis=1)
    key_parts = []
    value_parts = []
    for which_head in range(heads_here):
        score_cols = score_grads[which_head]
        prob_cols = prob_list[which_head]
        key_parts.append(contract_rows(score_cols, take_head(queries_held, which_head)))
        value_parts.append(contract_rows(prob_cols, take_head(grad_held, which_head)))
    summed = lax.psum_scatter(
        jnp.concatenate(key_parts + value_parts, axis=1), "frame", scatter_dimension=0, tiled=True
    )
    grad_keys = summed[:, :width_here].astype(jnp.bfloat16)
    grad_values = summed[:, width_here:].astype(jnp.bfloat16)
    grad_wq_local = contract_rows(features, grad_queries)
    grad_wk_local = contract_rows(features, grad_keys)
    grad_wv_local = contract_rows(features, grad_values)
    grad_wo_local = contract_rows(attended_all, upstream)
    back_part = jnp.dot(grad_queries, w_query.T, preferred_element_type=jnp.float32)
    back_part = back_part + jnp.dot(grad_keys, w_key.T, preferred_element_type=jnp.float32)
    back_part = back_part + jnp.dot(grad_values, w_value.T, preferred_element_type=jnp.float32)
    head_sum = lax.psum(back_part, "head")
    grad_features = (head_sum + upstream.astype(jnp.float32)).astype(jnp.bfloat16)
    grad_rim = frame_rims(grad_features)
    grad_wt = jnp.stack(
        [
            contract_rows(
                hidden_rim[offset * frame_len : offset * frame_len + tok_local], grad_features
            )
            for offset in range(3)
        ]
    )
    grad_hidden = jnp.zeros((tok_local, channels), jnp.float32)
    for offset in range(3):
        grad_hidden = grad_hidden + jnp.dot(
            grad_rim[(2 - offset) * frame_len : (2 - offset) * frame_len + tok_local],
            w_temporal[offset].T,
            preferred_element_type=jnp.float32,
        )
    grad_pre = (grad_hidden * silu_slope(pre_act)).astype(jnp.bfloat16)
    grad_ws = jnp.stack([contract_rows(taps[offset], grad_pre) for offset in range(9)])
    totals = lax.psum(
        (grad_ws, grad_wt, grad_wq_local, grad_wk_local, grad_wv_local, grad_wo_local),
        ("frame", "dp"),
    )
    factor = float(lax.axis_size("dp") * lax.axis_size("frame") * tok_local) ** (-0.5)
    return (
        totals[0] * factor,
        totals[1] * factor,
        totals[2] * factor,
        totals[3] * factor,
        totals[4] * factor,
        totals[5] * factor,
    )


def solution(mesh):
    in_specs = (
        P("dp", "frame", None),
        P("dp", None),
        P(),
        P(),
        P(None, "head"),
        P(None, "head"),
        P(None, "head"),
        P("head", None),
        P("dp", "frame", None),
    )
    out_specs = (P(), P(), P(None, "head"), P(None, "head"), P(None, "head"), P("head", None))
    return jax.shard_map(
        on_device, mesh=mesh, in_specs=in_specs, out_specs=out_specs, check_vma=False
    )
```

profile of v0, /device:TPU:8, one launch (start us, length us, event | category | flops | bytes accessed | tf_op | source)
XLA Modules:
  0.0 700.0 jit_solution(11616659482293236148)
XLA Ops:
  7.2 1.9 pad_slice_fusion
  9.2 1.2 fusion.60
  10.4 1.1 convolution_add_fusion.11
  13.6 4.0 collective-permute-start
  17.6 1.3 collective-permute-start.1
  19.1 4.3 collective-permute-done.1
  24.8 1.7 convolution_convert_fusion
  27.7 85.4 %all-gather.3.cloned.1.call-done = bf16[4096,256]{1,0:T(8,128)(2,1)} async-done(((bf16[256,256]{1,0:T(8,128)(2,1)}), bf16[4096,256]{1,0:T(8,128)(2,1)}) %all-gather.3.cloned.1.call-update) | async-done | bytes 2097168 | tf_op jit(solution)/shard_map/all_gather | solution.py:90
  113.1 2.3 fusion.108
  116.3 1.9 fusion.6
  118.7 2.4 fusion.9
  121.1 1.3 copy-done.1
  122.4 1.8 fusion.91
  124.2 1.8 fusion.94
  126.0 72.5 %all-gather.5.cloned.1.call-done = bf16[4096,256]{1,0:T(8,128)(2,1)} async-done(((bf16[256,256]{1,0:T(8,128)(2,1)}), bf16[4096,256]{1,0:T(8,128)(2,1)}) %all-gather.5.cloned.1.call-update) | async-done | bytes 2097168 | tf_op jit(solution)/shard_map/all_gather | solution.py:91
  198.4 2.8 convolution_convert_fusion.5
  201.3 2.9 multiply_reduce_fusion.1
  204.3 1.7 fusion.5
  206.5 1.7 copy-done.4
  208.1 1.7 fusion.4
  209.8 1.3 copy-done.2
  211.6 1.1 copy-done.7
  213.4 3.8 pad_maximum_fusion
  217.4 2.8 convolution_convert_fusion.6
  223.3 216.4 %reduce-scatter.2.cloned.1.call-done = f32[256,512]{0,1:T(8,128)} async-done(((f32[4096,512]{0,1:T(8,128)}), f32[256,512]{0,1:T(8,128)}) %reduce-scatter.2.cloned.1.call-update) | async-done | bytes 524304 | tf_op jit(solution)/shard_map/reduce_scatter | solution.py:147
  439.7 1.1 convert.4
  443.9 60.5 %all-reduce.5.cloned.1.call-done = f32[256,256]{1,0:T(8,128)} async-done(((f32[256,256]{1,0:T(8,128)}), f32[256,256]{1,0:T(8,128)}) %all-reduce.5.cloned.1.call-update) | async-done | bytes 262160 | tf_op jit(solution)/shard_map/psum | solution.py:159
  505.8 1.3 collective-permute-start.2
  507.1 4.5 collective-permute-start.3
  515.8 1.4 copy-done.9
  517.3 168.9 %all-reduce.7.cloned.1.call-done = (f32[9,256,256]{2,1,0:T(8,128)}, f32[3,256,256]{2,1,0:T(8,128)}, f32[256,256]{1,0:T(8,128)}, f32[256,256]{1,0:T(8,128)}, f32[256,256]{1,0:T(8,128)}, /*index=5*/f32[256,256]{1,0:T(8,128)}) async-done(((f32[9,256,256]{2,1,0:T(8,128)}, f32[3,256,256]{2,1,0:T(8,128)}, f32[256,256]{1,0:T(8,128)}, f32[256,256]{1,0:T(8,128)}, f32[256,256]{1,0:T(8,128)}, ...) | async-done | bytes 4194320 | tf_op jit(solution)/shard_map/psum | solution.py:179
  686.1 3.4 broadcast_multiply_fusion
  (158 shorter events, 23.3 us)
Async XLA Ops:
  7.2 20.4 %copy-start = (bf16[256,256]{1,0:T(8,128)(2,1)S(1)}, bf16[256,256]{1,0:T(8,128)(2,1)}, u32[]{:S(2)}) copy-start(bf16[256,256]{1,0:T(8,128)(2,1)} %param.13) | copy-start | bytes 393220
  7.2 4.7 copy-start.14
  7.2 4.3 copy-start.19
  7.2 105.9 %all-gather.3.cloned.1.call-start = ((), (), s32[]{:S(2)}) async-start(), calls=%async_computation.1 | async-start | bytes 2228224 | tf_op jit(solution)/shard_map/all_gather | solution.py:90
  11.9 7.0 %copy-start.17 = (bf16[3,256,256]{2,1,0:T(8,128)(2,1)S(1)}, bf16[3,256,256]{2,1,0:T(8,128)(2,1)}, u32[]{:S(2)}) copy-start(bf16[3,256,256]{2,1,0:T(8,128)(2,1)} %param.12) | copy-start | bytes 1179652
  12.5 11.3 %copy-start.27 = (bf16[256,256]{1,0:T(8,128)(2,1)S(1)}, bf16[256,256]{1,0:T(8,128)(2,1)}, u32[]{:S(2)}) copy-start(bf16[256,256]{1,0:T(8,128)(2,1)} %param.14) | copy-start | bytes 393220
  12.7 13.9 %copy-start.42 = (s32[1,4096]{1,0:T(1,128)S(1)}, s32[1,4096]{1,0:T(1,128)}, u32[]{:S(2)}) copy-start(s32[1,4096]{1,0:T(1,128)} %param.10) | copy-start | bytes 49156
  12.7 13.9 %copy-start.13 = (bf16[1,256,256]{2,1,0:T(8,128)(2,1)S(1)}, bf16[1,256,256]{2,1,0:T(8,128)(2,1)}, u32[]{:S(2)}) copy-start(bf16[1,256,256]{2,1,0:T(8,128)(2,1)} %param.17) | copy-start | bytes 393220
  13.6 13.0 %copy-start.37 = (bf16[256,256]{1,0:T(8,128)(2,1)S(1)}, bf16[256,256]{1,0:T(8,128)(2,1)}, u32[]{:S(2)}) copy-start(bf16[256,256]{1,0:T(8,128)(2,1)} %param.16) | copy-start | bytes 393220
  13.6 10.0 %collective-permute-start = (bf16[64,256]{1,0:T(8,128)(2,1)S(1)}, bf16[64,256]{1,0:T(8,128)(2,1)S(1)}, u32[]{:S(2)}, u32[]{:S(2)}) collective-permute-start(bf16[64,256]{1,0:T(8,128)(2,1)S(1)} %get-tuple-element.18), channel_id=1, source_target_pairs={{0,16},{16,32},{32,48},{48,64},{64,80},{80,96},{96,112},{112,128},... | collective-permute-start | bytes 98312 | tf_op jit(solution)/shard_map/ppermute | solution.py:19
  17.6 5.8 collective-permute-start.1
  23.4 91.9 %copy-start.38 = (bf16[64,256]{1,0:T(8,128)(2,1)}, bf16[64,256]{1,0:T(8,128)(2,1)S(1)}, u32[]{:S(2)}) copy-start(bf16[64,256]{1,0:T(8,128)(2,1)S(1)} %collective-permute-done.1) | copy-start | bytes 98308
  23.6 91.7 %copy-start.40 = (bf16[64,256]{1,0:T(8,128)(2,1)}, bf16[64,256]{1,0:T(8,128)(2,1)S(1)}, u32[]{:S(2)}) copy-start(bf16[64,256]{1,0:T(8,128)(2,1)S(1)} %collective-permute-done) | copy-start | bytes 98308
  24.7 173.7 %all-gather.5.cloned.1.call-start = ((), (), s32[]{:S(2)}) async-start(), calls=%async_computation.2 | async-start | bytes 2228224 | tf_op jit(solution)/shard_map/all_gather | solution.py:91
  26.5 413.2 %reduce-scatter.2.cloned.1.call-start = ((), (), s32[]{:S(2)}) async-start(), calls=%async_computation.3 | async-start | bytes 8912896 | tf_op jit(solution)/shard_map/reduce_scatter | solution.py:147
  26.6 89.7 %copy-start.43 = (s32[1,256]{1,0:T(1,128)}, s32[1,256]{1,0:T(1,128)S(1)}, u32[]{:S(2)}) copy-start(s32[1,256]{1,0:T(1,128)S(1)} %constant_dynamic-slice_fusion) | copy-start | bytes 3076
  27.7 87.6 %copy-start.25 = (bf16[256,256]{1,0:T(8,128)(2,1)}, bf16[256,256]{1,0:T(8,128)(2,1)S(1)}, u32[]{:S(2)}) copy-start(bf16[256,256]{1,0:T(8,128)(2,1)S(1)} %convolution_convert_fusion.3) | copy-start | bytes 393220
  198.4 5.8 copy-start.6
  201.3 4.7 copy-start.23
  217.2 287.1 %all-reduce.5.cloned.1.call-start = ((), (), s32[]{:S(2)}) async-start(), calls=%async_computation.4 | async-start | bytes 524288 | tf_op jit(solution)/shard_map/psum | solution.py:159
  221.2 220.5 %copy-start.28 = (bf16[256,256]{1,0:T(8,128)(2,1)S(1)}, bf16[256,256]{1,0:T(8,128)(2,1)}, u32[]{:S(2)}) copy-start(bf16[256,256]{1,0:T(8,128)(2,1)} %param.14) | copy-start | bytes 393220
  221.2 220.8 %copy-start.29 = (bf16[256,256]{1,0:T(8,128)(2,1)S(1)}, bf16[256,256]{1,0:T(8,128)(2,1)}, u32[]{:S(2)}) copy-start(bf16[256,256]{1,0:T(8,128)(2,1)} %param.15) | copy-start | bytes 393220
  223.3 282.3 %copy-start.18 = (bf16[3,256,256]{2,1,0:T(8,128)(2,1)S(1)}, bf16[3,256,256]{2,1,0:T(8,128)(2,1)}, u32[]{:S(2)}) copy-start(bf16[3,256,256]{2,1,0:T(8,128)(2,1)} %param.12) | copy-start | bytes 1179652
  440.8 70.9 %copy-start.41 = (bf16[64,256]{1,0:T(8,128)(2,1)S(1)}, bf16[64,256]{1,0:T(8,128)(2,1)}, u32[]{:S(2)}) copy-start(bf16[64,256]{1,0:T(8,128)(2,1)} %copy-done.40) | copy-start | bytes 98308
  441.7 70.2 %copy-start.39 = (bf16[64,256]{1,0:T(8,128)(2,1)S(1)}, bf16[64,256]{1,0:T(8,128)(2,1)}, u32[]{:S(2)}) copy-start(bf16[64,256]{1,0:T(8,128)(2,1)} %copy-done.38) | copy-start | bytes 98308
  442.9 243.2 %all-reduce.7.cloned.1.call-start = ((), (), s32[]{:S(2)}) async-start(), calls=%async_computation.5 | async-start | bytes 8388608 | tf_op jit(solution)/shard_map/psum | solution.py:179
  443.9 69.6 %copy-start.49 = (f32[256,256]{1,0:T(8,128)S(1)}, f32[256,256]{1,0:T(8,128)}, u32[]{:S(2)}) copy-start(f32[256,256]{1,0:T(8,128)} %get-tuple-element.31) | copy-start | bytes 786436
  505.8 7.7 %collective-permute-start.2 = (bf16[64,256]{1,0:T(8,128)(2,1)S(1)}, bf16[64,256]{1,0:T(8,128)(2,1)S(1)}, u32[]{:S(2)}, u32[]{:S(2)}) collective-permute-start(bf16[64,256]{1,0:T(8,128)(2,1)S(1)} %get-tuple-element.16), channel_id=1, source_target_pairs={{16,0},{32,16},{48,32},{64,48},{80,64},{96,80},{112,96},{128,112},... | collective-permute-start | bytes 98312 | tf_op jit(solution)/shard_map/ppermute | solution.py:21
  507.1 6.1 collective-permute-start.3
  686.1 4.9 copy-start.33
  686.1 5.6 copy-start.32
  686.1 6.3 copy-start.22
  (27 other events, 67.7 us)
Sparse Core Ops, SparseCore 0:
  24.8 88.2 all-gather.2
  116.2 82.1 all-gather.4
  217.3 222.3 reduce-scatter.1
  443.1 61.2 all-reduce.4
  517.4 168.7 all-reduce.6
where the time goes:
time: 700 us
  waiting for transfers between devices  608 us (87%)
  matrix products  37.3 us (5%)
  other arithmetic  18.4 us (3%)
  between operations  14.7 us (2%)
  starting transfers between devices  11.5 us (2%)
  local copies, waits for them, and re-layouts  9.96 us (1%)
    reduce_scatter x1, waiting for transfers between devices, on_device(): lax.psum_scatter(jnp.concatenate(key_parts + value_parts, axis=1), 'frame...  216 us
    psum x1, waiting for transfers between devices, on_device(): lax.psum((grad_ws, grad_wt, grad_wq_local, grad_wk_local, grad_wv_local,...  169 us
    all_gather x1, waiting for transfers between devices, on_device(): lax.all_gather(keys_local, 'frame', axis=0, tiled=True)  85.4 us
    all_gather x1, waiting for transfers between devices, on_device(): lax.all_gather(values_local, 'frame', axis=0, tiled=True)  72.5 us
    psum x1, waiting for transfers between devices, on_device(): head_sum = lax.psum(back_part, 'head')  60.5 us
  transfers between devices with their start and end apart: 9, of which 7 were waited for; matrix products, arithmetic and copies ran while one was open for 3% of the time, Pallas kernels for 0%

commit v1 on v0

--- a/solution.py
+++ b/solution.py
@@ -156,7 +156,13 @@
     back_part = jnp.dot(grad_queries, w_query.T, preferred_element_type=jnp.float32)
     back_part = back_part + jnp.dot(grad_keys, w_key.T, preferred_element_type=jnp.float32)
     back_part = back_part + jnp.dot(grad_values, w_value.T, preferred_element_type=jnp.float32)
-    head_sum = lax.psum(back_part, "head")
+    size = lax.axis_size("head")
+    head_sum, far = (back_part, 1)
+    while far < size:
+        head_sum = head_sum + lax.ppermute(
+            head_sum, "head", [(i_2, i_2 ^ far) for i_2 in range(size)]
+        )
+        far = 2 * far
     grad_features = (head_sum + upstream.astype(jnp.float32)).astype(jnp.bfloat16)
     grad_rim = frame_rims(grad_features)
     grad_wt = jnp.stack(

time: 700 us -> 656 us (0.937)
  waiting for transfers between devices: 608 us -> 560 us
    psum x1 -> x0, waiting for transfers between devices: 60.5 us -> none  [on_device(): head_sum = lax.psum(back_part, 'head')]
    ppermute x0 -> x3, waiting for transfers between devices: none -> 12.3 us  [on_device(): lax.ppermute(head_sum, 'head', [(i_2, i_2 ^ far) for i_2 in range(size)])]
  transfers between devices with their start and end apart: 9 -> 11, of which waited for: 7 -> 9; matrix products, arithmetic and copies ran while one was open for 3% -> 4% of each run, Pallas kernels for 0% -> 0%
where the time goes in v1:
time: 656 us; the launch traced here: 655 us
  waiting for transfers between devices  560 us (85%)
  matrix products  38.4 us (6%)
  other arithmetic  17.5 us (3%)
  between operations  14.7 us (2%)
  starting transfers between devices  14.6 us (2%)
  local copies, waits for them, and re-layouts  10.6 us (2%)
    reduce_scatter x1, waiting for transfers between devices, on_device(): lax.psum_scatter(jnp.concatenate(key_parts + value_parts, axis=1), 'frame...  218 us
    psum x1, waiting for transfers between devices, on_device(): lax.psum((grad_ws, grad_wt, grad_wq_local, grad_wk_local, grad_wv_local,...  167 us
    all_gather x1, waiting for transfers between devices, on_device(): lax.all_gather(keys_local, 'frame', axis=0, tiled=True)  85.4 us
    all_gather x1, waiting for transfers between devices, on_device(): lax.all_gather(values_local, 'frame', axis=0, tiled=True)  72.5 us
  transfers between devices with their start and end apart: 11, of which 9 were waited for; matrix products, arithmetic and copies ran while one was open for 4% of the time, Pallas kernels for 0%

profile of v1, /device:TPU:8, one launch (start us, length us, event | category | flops | bytes accessed | tf_op | source)
XLA Modules:
  0.0 655.4 jit_solution(4069861680038425393)
XLA Ops:
  7.2 1.9 pad_slice_fusion
  9.2 1.2 fusion.60
  13.6 4.0 collective-permute-start
  17.6 1.3 collective-permute-start.1
  19.1 4.3 collective-permute-done.1
  24.8 1.7 convolution_convert_fusion
  27.7 85.4 %all-gather.3.cloned.1.call-done = bf16[4096,256]{1,0:T(8,128)(2,1)} async-done(((bf16[256,256]{1,0:T(8,128)(2,1)}), bf16[4096,256]{1,0:T(8,128)(2,1)}) %all-gather.3.cloned.1.call-update) | async-done | bytes 2097168 | tf_op jit(solution)/shard_map/all_gather | solution.py:90
  113.1 2.3 fusion.108
  116.3 1.9 fusion.6
  118.7 2.4 fusion.9
  121.2 1.3 copy-done.1
  122.5 1.7 fusion.91
  124.2 1.7 fusion.94
  126.0 72.5 %all-gather.5.cloned.1.call-done = bf16[4096,256]{1,0:T(8,128)(2,1)} async-done(((bf16[256,256]{1,0:T(8,128)(2,1)}), bf16[4096,256]{1,0:T(8,128)(2,1)}) %all-gather.5.cloned.1.call-update) | async-done | bytes 2097168 | tf_op jit(solution)/shard_map/all_gather | solution.py:91
  198.4 2.8 convolution_convert_fusion.5
  201.3 2.9 multiply_reduce_fusion.1
  204.3 1.7 fusion.5
  206.5 1.7 copy-done.4
  208.1 1.7 fusion.4
  209.8 1.3 copy-done.2
  213.4 3.8 pad_maximum_fusion
  217.4 2.8 convolution_convert_fusion.6
  222.1 217.6 %reduce-scatter.2.cloned.1.call-done = f32[256,512]{0,1:T(8,128)} async-done(((f32[4096,512]{0,1:T(8,128)}), f32[256,512]{0,1:T(8,128)}) %reduce-scatter.2.cloned.1.call-update) | async-done | bytes 524304 | tf_op jit(solution)/shard_map/reduce_scatter | solution.py:147
  443.2 1.5 collective-permute-done.2
  447.3 5.9 collective-permute-done.3
  453.2 2.3 collective-permute-start.4
  457.4 4.9 collective-permute-done.4
  462.9 1.3 collective-permute-start.5
  464.2 4.5 collective-permute-start.6
  472.9 1.4 copy-done.9
  474.3 167.2 %all-reduce.4.cloned.1.call-done = (f32[9,256,256]{2,1,0:T(8,128)}, f32[3,256,256]{2,1,0:T(8,128)}, f32[256,256]{1,0:T(8,128)}, f32[256,256]{1,0:T(8,128)}, f32[256,256]{1,0:T(8,128)}, /*index=5*/f32[256,256]{1,0:T(8,128)}) async-done(((f32[9,256,256]{2,1,0:T(8,128)}, f32[3,256,256]{2,1,0:T(8,128)}, f32[256,256]{1,0:T(8,128)}, f32[256,256]{1,0:T(8,128)}, f32[256,256]{1,0:T(8,128)}, ...) | async-done | bytes 4194320 | tf_op jit(solution)/shard_map/psum | solution.py:185
  641.6 3.4 broadcast_multiply_fusion
  (167 shorter events, 28.2 us)
Async XLA Ops:
  7.2 20.4 %copy-start = (bf16[256,256]{1,0:T(8,128)(2,1)S(1)}, bf16[256,256]{1,0:T(8,128)(2,1)}, u32[]{:S(2)}) copy-start(bf16[256,256]{1,0:T(8,128)(2,1)} %param.13) | copy-start | bytes 393220
  7.2 105.9 %all-gather.3.cloned.1.call-start = ((), (), s32[]{:S(2)}) async-start(), calls=%async_computation.1 | async-start | bytes 2228224 | tf_op jit(solution)/shard_map/all_gather | solution.py:90
  11.9 7.0 %copy-start.17 = (bf16[3,256,256]{2,1,0:T(8,128)(2,1)S(1)}, bf16[3,256,256]{2,1,0:T(8,128)(2,1)}, u32[]{:S(2)}) copy-start(bf16[3,256,256]{2,1,0:T(8,128)(2,1)} %param.12) | copy-start | bytes 1179652
  12.5 11.3 %copy-start.31 = (bf16[256,256]{1,0:T(8,128)(2,1)S(1)}, bf16[256,256]{1,0:T(8,128)(2,1)}, u32[]{:S(2)}) copy-start(bf16[256,256]{1,0:T(8,128)(2,1)} %param.14) | copy-start | bytes 393220
  12.7 13.9 %copy-start.44 = (s32[1,4096]{1,0:T(1,128)S(1)}, s32[1,4096]{1,0:T(1,128)}, u32[]{:S(2)}) copy-start(s32[1,4096]{1,0:T(1,128)} %param.10) | copy-start | bytes 49156
  12.7 13.9 %copy-start.13 = (bf16[1,256,256]{2,1,0:T(8,128)(2,1)S(1)}, bf16[1,256,256]{2,1,0:T(8,128)(2,1)}, u32[]{:S(2)}) copy-start(bf16[1,256,256]{2,1,0:T(8,128)(2,1)} %param.17) | copy-start | bytes 393220
  13.6 13.0 %copy-start.39 = (bf16[256,256]{1,0:T(8,128)(2,1)S(1)}, bf16[256,256]{1,0:T(8,128)(2,1)}, u32[]{:S(2)}) copy-start(bf16[256,256]{1,0:T(8,128)(2,1)} %param.16) | copy-start | bytes 393220
  13.6 10.0 %collective-permute-start = (bf16[64,256]{1,0:T(8,128)(2,1)S(1)}, bf16[64,256]{1,0:T(8,128)(2,1)S(1)}, u32[]{:S(2)}, u32[]{:S(2)}) collective-permute-start(bf16[64,256]{1,0:T(8,128)(2,1)S(1)} %get-tuple-element.18), channel_id=1, source_target_pairs={{0,16},{16,32},{32,48},{48,64},{64,80},{80,96},{96,112},{112,128},... | collective-permute-start | bytes 98312 | tf_op jit(solution)/shard_map/ppermute | solution.py:19
  17.6 5.8 collective-permute-start.1
  23.4 91.9 %copy-start.40 = (bf16[64,256]{1,0:T(8,128)(2,1)}, bf16[64,256]{1,0:T(8,128)(2,1)S(1)}, u32[]{:S(2)}) copy-start(bf16[64,256]{1,0:T(8,128)(2,1)S(1)} %collective-permute-done.1) | copy-start | bytes 98308
  23.6 91.7 %copy-start.42 = (bf16[64,256]{1,0:T(8,128)(2,1)}, bf16[64,256]{1,0:T(8,128)(2,1)S(1)}, u32[]{:S(2)}) copy-start(bf16[64,256]{1,0:T(8,128)(2,1)S(1)} %collective-permute-done) | copy-start | bytes 98308
  24.7 173.7 %all-gather.5.cloned.1.call-start = ((), (), s32[]{:S(2)}) async-start(), calls=%async_computation.2 | async-start | bytes 2228224 | tf_op jit(solution)/shard_map/all_gather | solution.py:91
  26.5 413.2 %reduce-scatter.2.cloned.1.call-start = ((), (), s32[]{:S(2)}) async-start(), calls=%async_computation.3 | async-start | bytes 8912896 | tf_op jit(solution)/shard_map/reduce_scatter | solution.py:147
  26.6 89.7 %copy-start.45 = (s32[1,256]{1,0:T(1,128)}, s32[1,256]{1,0:T(1,128)S(1)}, u32[]{:S(2)}) copy-start(s32[1,256]{1,0:T(1,128)S(1)} %constant_dynamic-slice_fusion) | copy-start | bytes 3076
  27.7 87.6 %copy-start.29 = (bf16[256,256]{1,0:T(8,128)(2,1)}, bf16[256,256]{1,0:T(8,128)(2,1)S(1)}, u32[]{:S(2)}) copy-start(bf16[256,256]{1,0:T(8,128)(2,1)S(1)} %convolution_convert_fusion.3) | copy-start | bytes 393220
  198.4 5.8 copy-start.6
  217.2 424.3 %all-reduce.4.cloned.1.call-start = ((), (), s32[]{:S(2)}) async-start(), calls=%async_computation.4 | async-start | bytes 8388608 | tf_op jit(solution)/shard_map/psum | solution.py:185
  221.8 224.6 %copy-start.24 = (bf16[256,128]{0,1:T(8,128)(2,1)S(1)}, bf16[256,128]{0,1:T(8,128)(2,1)}, u32[]{:S(2)}) copy-start(bf16[256,128]{0,1:T(8,128)(2,1)} %copy-done.23) | copy-start | bytes 196612
  221.8 224.6 %copy-start.38 = (bf16[256,128]{0,1:T(8,128)(2,1)S(1)}, bf16[256,128]{0,1:T(8,128)(2,1)}, u32[]{:S(2)}) copy-start(bf16[256,128]{0,1:T(8,128)(2,1)} %get-tuple-element.36) | copy-start | bytes 196612
  222.1 223.4 %copy-start.26 = (bf16[256,128]{0,1:T(8,128)(2,1)S(1)}, bf16[256,128]{0,1:T(8,128)(2,1)}, u32[]{:S(2)}) copy-start(bf16[256,128]{0,1:T(8,128)(2,1)} %copy-done.25) | copy-start | bytes 196612
  222.1 223.4 %copy-start.28 = (bf16[256,128]{0,1:T(8,128)(2,1)S(1)}, bf16[256,128]{0,1:T(8,128)(2,1)}, u32[]{:S(2)}) copy-start(bf16[256,128]{0,1:T(8,128)(2,1)} %copy-done.27) | copy-start | bytes 196612
  443.1 1.6 collective-permute-start.2
  444.7 17.9 %copy-start.18 = (bf16[3,256,256]{2,1,0:T(8,128)(2,1)S(1)}, bf16[3,256,256]{2,1,0:T(8,128)(2,1)}, u32[]{:S(2)}) copy-start(bf16[3,256,256]{2,1,0:T(8,128)(2,1)} %param.12) | copy-start | bytes 1179652
  444.8 24.0 %copy-start.43 = (bf16[64,256]{1,0:T(8,128)(2,1)S(1)}, bf16[64,256]{1,0:T(8,128)(2,1)}, u32[]{:S(2)}) copy-start(bf16[64,256]{1,0:T(8,128)(2,1)} %copy-done.42) | copy-start | bytes 98308
  444.8 8.4 %collective-permute-start.3 = (f32[256,256]{1,0:T(8,128)S(1)}, f32[256,256]{1,0:T(8,128)S(1)}, u32[]{:S(2)}, u32[]{:S(2)}) collective-permute-start(f32[256,256]{1,0:T(8,128)S(1)} %add.113), channel_id=1, source_target_pairs={{0,4},{2,6},{4,0},{6,2},{8,12},{10,14},{12,8},{14,10},{1,5},{3,7},... | collective-permute-start | bytes 786440 | tf_op jit(solution)/shard_map/ppermute | solution.py:162
  446.4 22.6 %copy-start.41 = (bf16[64,256]{1,0:T(8,128)(2,1)S(1)}, bf16[64,256]{1,0:T(8,128)(2,1)}, u32[]{:S(2)}) copy-start(bf16[64,256]{1,0:T(8,128)(2,1)} %copy-done.40) | copy-start | bytes 98308
  453.2 9.1 %collective-permute-start.4 = (f32[256,256]{1,0:T(8,128)S(1)}, f32[256,256]{1,0:T(8,128)S(1)}, u32[]{:S(2)}, u32[]{:S(2)}) collective-permute-start(f32[256,256]{1,0:T(8,128)S(1)} %add.114), channel_id=1, source_target_pairs={{0,8},{2,10},{4,12},{6,14},{8,0},{10,2},{12,4},{14,6},{1,9},{3,11}... | collective-permute-start | bytes 786440 | tf_op jit(solution)/shard_map/ppermute | solution.py:162
  462.4 8.2 %copy-start.51 = (f32[256,256]{1,0:T(8,128)S(1)}, f32[256,256]{1,0:T(8,128)}, u32[]{:S(2)}) copy-start(f32[256,256]{1,0:T(8,128)} %get-tuple-element.31) | copy-start | bytes 786436
  462.9 7.7 %collective-permute-start.5 = (bf16[64,256]{1,0:T(8,128)(2,1)S(1)}, bf16[64,256]{1,0:T(8,128)(2,1)S(1)}, u32[]{:S(2)}, u32[]{:S(2)}) collective-permute-start(bf16[64,256]{1,0:T(8,128)(2,1)S(1)} %get-tuple-element.16), channel_id=1, source_target_pairs={{16,0},{32,16},{48,32},{64,48},{80,64},{96,80},{112,96},{128,112},... | collective-permute-start | bytes 98312 | tf_op jit(solution)/shard_map/ppermute | solution.py:21
  464.2 6.1 collective-permute-start.6
  641.6 5.6 copy-start.34
  641.6 6.3 copy-start.22
  (31 other events, 83.7 us)
Sparse Core Ops, SparseCore 0:
  24.8 88.2 all-gather.2
  116.2 82.1 all-gather.4
  217.3 222.3 reduce-scatter.1
  474.4 167.0 all-reduce.3
